TPU v7x, 32 devices: a whole 2x2x4 slice. The times are simulated.
32 devices in a mesh: row: 8 (over z, y), col: 4 (over x, core).
Axes of the slice: x: 2, y: 2, z: 4, core: 2. Of those that a mesh axis runs over, the one named last changes fastest.
Arguments:
- phase: float32 [512, 256, 512], P(None, 'row', 'col'), may hold values from -24 to 24
- pairs: int32 [512, 2], replicated, may hold values from 0 to 127, as said below
Outputs:
- solution: float32 [128, 256, 512], P(None, 'row', 'col')
Inputs may be any that keep to these rules, and one draw needn't show every extreme that they name: `pairs`: each row holds two different dates, the earlier one first.
All inputs are finite; a program needn't handle non-finite values.
Results may differ from a plain program's by a relative error of at most 0.00018.
Values sent between devices are 32-bit elements; how exact they have to be, the bound alone decides.
A program may use at most 128 MiB of HBM per device.

v0:
```python
import functools

import jax
import jax.numpy as jnp
from jax import lax
from jax.experimental import pallas as pl
from jax.experimental.pallas import tpu as pltpu
from jax.sharding import PartitionSpec as P

ND = 128
ITERS = 3
LAM = 0.8

MESH = pl.DeviceIdType.MESH
STEPS = ((-1, 0), (1, 0), (0, -1), (0, 1), (1, 1), (1, -1), (-1, 1), (-1, -1))


def split(x):
    high = x.astype(jnp.bfloat16)
    return high, (x - high.astype(jnp.float32)).astype(jnp.bfloat16)


def folded(x):
    return jnp.sum(x.reshape(x.shape[0] // 8, 8, x.shape[1]), axis=0)


def inverse(x):
    return jnp.where(x > 0.0, 1.0 / x, 0.0)


def coefficients(mu, beta, shift, scale):
    def inner(p, q, off=0):
        total = 0.0
        for i, a in enumerate(p):
            for j, b in enumerate(q):
                total = total + a * b * mu[i + j + off]
        return total

    zero = jnp.zeros_like(beta)
    alpha = jnp.sqrt(mu[0]) / beta
    vec = [1.0 / (alpha * beta)]
    before, coupling, theta = [zero], zero, zero
    search, phi_bar, total = [zero], beta, [zero] * ITERS
    rho, phi = None, None
    for step in range(ITERS):
        mean = inner(vec, vec, 1)
        rho_sq = scale * mean + shift * inner(vec, vec) - theta * theta
        inv_rho = inverse(jnp.sqrt(jnp.maximum(rho_sq, 0.0)))
        if step == 0:
            phi = alpha * phi_bar * inv_rho
            search = vec
        else:
            phi = -theta * phi * inv_rho
            past = search + [zero] * (len(vec) - len(search))
            search = [a - theta * inv_before * b for a, b in zip(vec, past)]
        for i, a in enumerate(search):
            total[i] = total[i] + phi * inv_rho * a
        if step < ITERS - 1:
            up = [zero] + vec
            mid = vec + [zero]
            low = before + [zero] * (len(up) - len(before))
            nxt = [a - mean * b - coupling * c for a, b, c in zip(up, mid, low)]
            coupling = jnp.sqrt(jnp.maximum(inner(nxt, nxt), 0.0))
            before = vec
            vec = [a * inverse(coupling) for a in nxt]
            theta = scale * coupling * inv_rho
            inv_before = inv_rho
    return total


def kernel(dims, phase, pairs, out, held, v0, v1, v2, side, side_t, from_left, from_right,
           corner, beside, temp, acc, mine, cols_in, part, rows_in, load_sem, send_sem, recv_sem,
           col_send, col_recv, row_send, row_recv):
    n_row, n_col, count, rows, cols = dims
    tiles, pairs_of_rows = rows // 8, rows // 2
    vecs = (v0, v1, v2)
    row, col = lax.axis_index("row"), lax.axis_index("col")

    loads = [
        pltpu.make_async_copy(phase.at[:, t], held.at[t], load_sem.at[t]) for t in range(tiles)
    ]
    order = [0, tiles - 1] + list(range(1, tiles - 1))
    for t in order:
        loads[t].start()

    def exists(dr, dc):
        ok = None
        for pos, step, n in ((row, dr, n_row), (col, dc, n_col)):
            if step:
                here = pos + step >= 0 if step < 0 else pos + step < n
                ok = here if ok is None else jnp.logical_and(ok, here)
        return ok

    barrier = pltpu.get_barrier_semaphore()
    for d in range(1, n_row):
        pl.semaphore_signal(
            barrier, inc=1, device_id=(lax.rem(row + d, n_row), col), device_id_type=MESH
        )
    for d in range(1, n_col):
        pl.semaphore_signal(
            barrier, inc=1, device_id=(row, lax.rem(col + d, n_col)), device_id_type=MESH
        )
    for dr, dc in STEPS[4:]:
        @pl.when(exists(dr, dc))
        def _():
            pl.semaphore_signal(
                barrier, inc=1, device_id=(row + dr, col + dc), device_id_type=MESH
            )

    def beside_count(pos, n):
        return jnp.where(pos > 0, 1, 0) + jnp.where(pos < n - 1, 1, 0)

    def meet():
        corners = beside_count(row, n_row) * beside_count(col, n_col)
        pl.semaphore_wait(barrier, n_row + n_col - 2 + corners)

    def message(k, i, receiving=False):
        dr, dc = STEPS[i]
        v = vecs[k]
        low, high = side_t.at[k, pl.ds(0, 8)], side_t.at[k, pl.ds(4 * rows - 8, 8)]
        src, dst = (
            (v.at[pl.ds(2, 2)], v.at[pl.ds(rows + 2, 2)]),
            (v.at[pl.ds(rows, 2)], v.at[pl.ds(0, 2)]),
            (side.at[k], from_right.at[k]),
            (side.at[k], from_left.at[k]),
            (high, corner.at[k, 0]),
            (high, corner.at[k, 1]),
            (low, corner.at[k, 2]),
            (low, corner.at[k, 3]),
        )[i]
        sign = -1 if receiving else 1
        return pltpu.make_async_remote_copy(
            src_ref=src, dst_ref=dst, send_sem=send_sem.at[k, i], recv_sem=recv_sem.at[k, i],
            device_id=(row + sign * dr, col + sign * dc), device_id_type=MESH,
        )

    def send(k, which):
        for i in which:
            @pl.when(exists(*STEPS[i]))
            def _():
                message(k, i).start()

    def receive(k, which):
        for i in which:
            dr, dc = STEPS[i]
            @pl.when(exists(-dr, -dc))
            def _():
                message(k, i, True).wait_recv()

    for i, (dr, dc) in enumerate(STEPS):
        @pl.when(jnp.logical_not(exists(-dr, -dc)))
        def _():
            for k in range(ITERS):
                if i == 0:
                    vecs[k][pl.ds(rows + 2, 2)] = jnp.zeros((2, ND, cols), jnp.float32)
                elif i == 1:
                    vecs[k][pl.ds(0, 2)] = jnp.zeros((2, ND, cols), jnp.float32)
                elif i == 2:
                    from_right[k] = jnp.zeros((ND, cols), jnp.float32)
                elif i == 3:
                    from_left[k] = jnp.zeros((ND, cols), jnp.float32)
                else:
                    corner[k, i - 4] = jnp.zeros((8, ND), jnp.float32)

    acc[...] = jnp.zeros_like(acc)
    lane = lax.broadcasted_iota(jnp.int32, (ND, cols), 1)

    dates = lax.broadcasted_iota(jnp.int32, (count, ND), 1)
    design = (dates == pairs[:, 1:2]).astype(jnp.float32) - (dates == pairs[:, 0:1]).astype(
        jnp.float32
    )
    pull = design.T.astype(jnp.bfloat16)
    gram = jnp.dot(pull, design.astype(jnp.bfloat16), preferred_element_type=jnp.float32)
    gram_high, gram_low = split(gram)
    normal = jnp.concatenate(
        [
            jnp.concatenate([gram_high, gram_high], axis=1),
            jnp.concatenate([gram_low, gram_low], axis=1),
        ],
        axis=0,
    )

    shift = 2.0 * count / ND + 20.0 * LAM * LAM
    scale = 0.75 * shift
    k2 = LAM * LAM / scale

    def put(k, r, x):
        vecs[k][r + 2] = x
        side[k] = jnp.where(lane // 4 == r, pltpu.roll(x, 4 * r + 2, 1), side[k])

    def pulled(t, p):
        flat = held.at[t].reshape(count * 8, cols)
        x = jnp.concatenate(
            [flat[pl.ds(2 * p + j, count, stride=8), :] for j in range(2)], axis=1
        )
        square = x * x
        acc[6] += folded(square[:, :cols] + square[:, cols:])
        high, low = split(x)
        b = jnp.dot(pull, high, preferred_element_type=jnp.float32) + jnp.dot(
            pull, low, preferred_element_type=jnp.float32
        )
        r = 8 * t + 2 * p
        put(0, r, b[:, :cols])
        put(0, r + 1, b[:, cols:])

    side[0] = jnp.zeros((ND, cols), jnp.float32)
    for n, t in enumerate(order):
        loads[t].wait()

        @pl.loop(0, 4)
        def _(p):
            pulled(t, p)

        if n == min(1, tiles - 1):
            meet()
            send(0, (0, 1))

    def finish_sides(k):
        send(k, (2, 3))
        side_t[k] = side[k].T
        send(k, (4, 5, 6, 7))

    finish_sides(0)

    sub = lax.broadcasted_iota(jnp.int32, (cols, ND), 0)
    col_out = jnp.where(jnp.logical_and(lane == 0, col == 0), 1.0, 0.0) + jnp.where(
        jnp.logical_and(lane == cols - 1, col == n_col - 1), 1.0, 0.0
    )

    def horizontal(x, y):
        return pltpu.roll(jnp.where(lane == cols - 1, y, x), 1, 1) + pltpu.roll(
            jnp.where(lane == 0, y, x), cols - 1, 1
        )

    for k in range(ITERS):
        v = vecs[k]
        last = k == ITERS - 1

        @pl.loop(0, pairs_of_rows)
        def _(p):
            r = 2 * p
            x = jnp.concatenate([v[r + 2], v[r + 3]], axis=1)
            both = jnp.concatenate(split(x), axis=0)
            y = jnp.dot(normal, both, preferred_element_type=jnp.float32)
            y = (y[:ND] + y[ND:]) * (1.0 / scale)
            temp[r] = y[:, :cols]
            temp[r + 1] = y[:, cols:]

        receive(k, (2, 3))
        side_in = jnp.where(lax.rem(lane, 4) < 2, from_left[k], from_right[k])
        from_left[k] = side_in

        @pl.loop(0, rows)
        def _(r):
            x = v[r + 2]
            y = pltpu.roll(from_left[k], lax.rem(2 * cols - 2 - 4 * r, cols), 1)
            h = horizontal(x, y)
            d2 = pltpu.roll(jnp.where(lane >= cols - 2, y, x), 2, 1) + pltpu.roll(
                jnp.where(lane < 2, y, x), cols - 2, 1
            )
            edge = jnp.where(jnp.logical_and(r == 0, row == 0), 1.0, 0.0) + jnp.where(
                jnp.logical_and(r == rows - 1, row == n_row - 1), 1.0, 0.0
            )
            centre = (20.0 * k2 - shift / scale) - k2 * (col_out + edge)
            beside[r + 1] = h
            temp[r] = temp[r] + centre * x + k2 * (d2 - 8.0 * h)

        receive(k, (0, 1, 4, 5, 6, 7))
        for at, h_at, left, right, a, b in (
            (1, 0, 0, 1, 5, 6),
            (rows + 2, rows + 1, 2, 3, 1, 2),
        ):
            m = jnp.where(
                sub == cols - 1,
                corner[k, left, pl.ds(a, 1), :],
                jnp.where(sub == 0, corner[k, right, pl.ds(b, 1), :], 0.0),
            )
            beside[h_at] = horizontal(v[at], m.T)

        if not last:
            side[k + 1] = jnp.zeros((ND, cols), jnp.float32)

        def both_rows(p):
            r = 2 * p
            x = [v[r + j] for j in range(6)]
            h = [beside[r + j] for j in range(4)]
            new = [
                temp[r + j]
                + k2 * (2.0 * (h[j] + h[j + 2]) + (x[j] + x[j + 4]) - 8.0 * (x[j + 1] + x[j + 3]))
                for j in range(2)
            ]
            if k == 0:
                acc[0] += folded(x[2] * x[2] + x[3] * x[3])
            acc[2 * k + 1] += folded(x[2] * new[0] + x[3] * new[1])
            if not last:
                acc[2 * k + 2] += folded(new[0] * new[0] + new[1] * new[1])
                put(k + 1, r, new[0])
                put(k + 1, r + 1, new[1])

        @pl.loop(0, 2)
        def _(e):
            both_rows(e * (pairs_of_rows - 1))

        if not last:
            send(k + 1, (0, 1))

        @pl.loop(1, pairs_of_rows - 1)
        def _(p):
            both_rows(p)

        if not last:
            finish_sides(k + 1)

    slot = lax.broadcasted_iota(jnp.int32, (8, cols), 0)
    local = jnp.zeros((8, cols), jnp.float32)
    for j in range(7):
        local = jnp.where(slot == j, jnp.sum(acc[j], axis=0, keepdims=True), local)

    def gather(source, into, send_s, recv_s, me, n, where_to):
        into[me] = source[...]
        copies = []
        for d in range(1, n):
            c = pltpu.make_async_remote_copy(
                src_ref=source, dst_ref=into.at[n + d], send_sem=send_s.at[d],
                recv_sem=recv_s.at[d], device_id=where_to(lax.rem(me + d, n)),
                device_id_type=MESH,
            )
            c.start()
            copies.append(c)
        for d, c in enumerate(copies, 1):
            c.wait()
            into[lax.rem(me + n - d, n)] = into[n + d]
        total = into[0]
        for i in range(1, n):
            total = total + into[i]
        return total

    mine[...] = local
    part[...] = gather(mine, cols_in, col_send, col_recv, col, n_col, lambda c: (row, c))
    sums = gather(part, rows_in, row_send, row_recv, row, n_row, lambda r: (r, col))
    sums = jnp.broadcast_to(jnp.sum(sums, axis=1, keepdims=True), (8, cols))
    mu = [sums[j : j + 1] for j in range(6)]
    y = coefficients(mu, jnp.sqrt(sums[6:7]), shift, scale)

    @pl.loop(0, rows)
    def _(r):
        out[pl.ds(r, ND, stride=rows), :] = y[0] * v0[r + 2] + y[1] * v1[r + 2] + y[2] * v2[r + 2]

    for k in range(ITERS):
        for i, step in enumerate(STEPS):
            @pl.when(exists(*step))
            def _():
                message(k, i).wait_send()


def on_device(n_row, n_col, phase, pairs):
    count, rows, cols = phase.shape
    assert rows % 8 == 0 and 4 * rows == cols and cols == ND
    f32 = jnp.float32
    dma = pltpu.SemaphoreType.DMA
    result = pl.pallas_call(
        functools.partial(kernel, (n_row, n_col, count, rows, cols)),
        out_shape=jax.ShapeDtypeStruct((ND * rows, cols), f32),
        in_specs=[pl.BlockSpec(memory_space=pl.ANY), pl.BlockSpec(memory_space=pltpu.VMEM)],
        out_specs=pl.BlockSpec(memory_space=pltpu.VMEM),
        scratch_shapes=[
            pltpu.VMEM((rows // 8, count, 8, cols), f32),
            pltpu.VMEM((rows + 4, ND, cols), f32),
            pltpu.VMEM((rows + 4, ND, cols), f32),
            pltpu.VMEM((rows + 4, ND, cols), f32),
            pltpu.VMEM((ITERS, ND, cols), f32),
            pltpu.VMEM((ITERS, cols, ND), f32),
            pltpu.VMEM((ITERS, ND, cols), f32),
            pltpu.VMEM((ITERS, ND, cols), f32),
            pltpu.VMEM((ITERS, 4, 8, ND), f32),
            pltpu.VMEM((rows + 2, ND, cols), f32),
            pltpu.VMEM((rows, ND, cols), f32),
            pltpu.VMEM((8, 8, cols), f32),
            pltpu.VMEM((8, cols), f32),
            pltpu.VMEM((2 * n_col, 8, cols), f32),
            pltpu.VMEM((8, cols), f32),
            pltpu.VMEM((2 * n_row, 8, cols), f32),
            dma((rows // 8,)),
            dma((ITERS, 8)),
            dma((ITERS, 8)),
            dma((n_col,)),
            dma((n_col,)),
            dma((n_row,)),
            dma((n_row,)),
        ],
        compiler_params=pltpu.CompilerParams(
            collective_id=0, has_side_effects=True, vmem_limit_bytes=48 * 1024 * 1024
        ),
    )(phase.reshape(count, rows // 8, 8, cols), pairs)
    return result.reshape(ND, rows, cols)


def solution(mesh):
    shape = mesh.shape
    return jax.shard_map(
        functools.partial(on_device, shape["row"], shape["col"]),
        mesh=mesh,
        in_specs=(P(None, "row", "col"), P()),
        out_specs=P(None, "row", "col"),
        check_vma=False,
    )
```

profile of v0, /device:TPU:0, one launch (start us, length us, event | category | flops | bytes accessed | tf_op | source)
XLA Modules:
  0.0 59.6 jit_solution(5023513172885218345)
XLA Ops:
  0.0 0.8 %copy.3.pairs = s32[512,2]{1,0:T(8,128)S(1)} copy(s32[512,2]{0,1:T(2,128)} %param.3) | data formatting | bytes 8192 | tf_op args[1]
  0.8 57.4 %shard_map.28 = f32[4096,128]{1,0:T(8,128)S(1)} custom-call(f32[512,4,8,128]{3,2,1,0:T(8,128)} %bitcast.3, s32[512,2]{1,0:T(8,128)S(1)} %copy.3.pairs), custom_call_target="tpu_custom_call" | custom-call | tf_op jit(solution)/shard_map/pallas_call | solution.py:361
  58.3 1.3 %copy.5 = f32[128,32,128]{2,1,0:T(8,128)} copy(f32[128,32,128]{2,1,0:T(8,128)S(1)} %bitcast.2) | data formatting | bytes 4194304
where the time goes:
time: 59.8 us; the launch traced here: 59.6 us
  Pallas kernels  57.4 us (96%)
  local copies, waits for them, and re-layouts  2.15 us (4%)
    pallas_call x1, Pallas kernels, on_device(): pl.pallas_call(functools.partial(kernel, (n_row, n_col, count, rows, cols...  57.4 us
    unnamed x2, local copies, waits for them, and re-layouts  2.15 us

commit v1 on v0

--- a/solution.py
+++ b/solution.py
@@ -165,12 +165,14 @@
     acc[...] = jnp.zeros_like(acc)
     lane = lax.broadcasted_iota(jnp.int32, (ND, cols), 1)
 
-    dates = lax.broadcasted_iota(jnp.int32, (count, ND), 1)
-    design = (dates == pairs[:, 1:2]).astype(jnp.float32) - (dates == pairs[:, 0:1]).astype(
+    dates = lax.broadcasted_iota(jnp.int32, (ND, count), 0)
+    pull = (dates == pairs[1:2, :]).astype(jnp.float32) - (dates == pairs[0:1, :]).astype(
         jnp.float32
     )
-    pull = design.T.astype(jnp.bfloat16)
-    gram = jnp.dot(pull, design.astype(jnp.bfloat16), preferred_element_type=jnp.float32)
+    pull = pull.astype(jnp.bfloat16)
+    gram = lax.dot_general(
+        pull, pull, (((1,), (1,)), ((), ())), preferred_element_type=jnp.float32
+    )
     gram_high, gram_low = split(gram)
     normal = jnp.concatenate(
         [
@@ -236,7 +238,7 @@
         v = vecs[k]
         last = k == ITERS - 1
 
-        @pl.loop(0, pairs_of_rows)
+        @pl.loop(0, pairs_of_rows, unroll=4)
         def _(p):
             r = 2 * p
             x = jnp.concatenate([v[r + 2], v[r + 3]], axis=1)
@@ -250,7 +252,7 @@
         side_in = jnp.where(lax.rem(lane, 4) < 2, from_left[k], from_right[k])
         from_left[k] = side_in
 
-        @pl.loop(0, rows)
+        @pl.loop(0, rows, unroll=4)
         def _(r):
             x = v[r + 2]
             y = pltpu.roll(from_left[k], lax.rem(2 * cols - 2 - 4 * r, cols), 1)
@@ -304,7 +306,7 @@
         if not last:
             send(k + 1, (0, 1))
 
-        @pl.loop(1, pairs_of_rows - 1)
+        @pl.loop(1, pairs_of_rows - 1, unroll=2)
         def _(p):
             both_rows(p)
 
@@ -342,7 +344,7 @@
     mu = [sums[j : j + 1] for j in range(6)]
     y = coefficients(mu, jnp.sqrt(sums[6:7]), shift, scale)
 
-    @pl.loop(0, rows)
+    @pl.loop(0, rows, unroll=4)
     def _(r):
         out[pl.ds(r, ND, stride=rows), :] = y[0] * v0[r + 2] + y[1] * v1[r + 2] + y[2] * v2[r + 2]
 
@@ -391,7 +393,7 @@
         compiler_params=pltpu.CompilerParams(
             collective_id=0, has_side_effects=True, vmem_limit_bytes=48 * 1024 * 1024
         ),
-    )(phase.reshape(count, rows // 8, 8, cols), pairs)
+    )(phase.reshape(count, rows // 8, 8, cols), pairs.T)
     return result.reshape(ND, rows, cols)
 
 

time: 59.8 us -> 50.9 us (0.85)
  Pallas kernels: 57.4 us -> 48.7 us
    pallas_call x1, Pallas kernels: 57.4 us -> 48.7 us  [on_device(): pl.pallas_call(functools.partial(kernel, (n_row, n_col, count, rows, cols...]
    unnamed x2 -> x3, local copies, waits for them, and re-layouts: 2.15 us -> 2.01 us
where the time goes in v1:
time: 50.9 us; the launch traced here: 50.8 us
  Pallas kernels  48.7 us (96%)
  local copies, waits for them, and re-layouts  2.01 us (4%)
    pallas_call x1, Pallas kernels, on_device(): pl.pallas_call(functools.partial(kernel, (n_row, n_col, count, rows, cols...  48.7 us
    unnamed x3, local copies, waits for them, and re-layouts  2.01 us

profile of v1, /device:TPU:0, one launch (start us, length us, event | category | flops | bytes accessed | tf_op | source)
XLA Modules:
  0.0 50.8 jit_solution(8041717056311717357)
XLA Ops:
  0.0 0.0 copy-start
  0.0 0.7 %copy-done = s32[512,2]{0,1:T(2,128)S(1)} copy-done((s32[512,2]{0,1:T(2,128)S(1)}, s32[512,2]{0,1:T(2,128)}, u32[]{:S(2)}) %copy-start) | copy-done | bytes 4120
  0.7 48.7 %shard_map.28 = f32[4096,128]{1,0:T(8,128)S(1)} custom-call(f32[512,4,8,128]{3,2,1,0:T(8,128)} %bitcast.5, s32[2,512]{1,0:T(2,128)S(1)} %bitcast.4), custom_call_target="tpu_custom_call" | custom-call | tf_op jit(solution)/shard_map/pallas_call | solution.py:363
  49.4 1.3 %copy.4 = f32[128,32,128]{2,1,0:T(8,128)} copy(f32[128,32,128]{2,1,0:T(8,128)S(1)} %bitcast.3) | data formatting | bytes 4194304
Async XLA Ops:
  0.0 0.7 %copy-start = (s32[512,2]{0,1:T(2,128)S(1)}, s32[512,2]{0,1:T(2,128)}, u32[]{:S(2)}) copy-start(s32[512,2]{0,1:T(2,128)} %param.3) | copy-start | bytes 12292

commit v2 on v1

--- a/solution.py
+++ b/solution.py
@@ -186,9 +186,14 @@
     scale = 0.75 * shift
     k2 = LAM * LAM / scale
 
-    def put(k, r, x):
-        vecs[k][r + 2] = x
-        side[k] = jnp.where(lane // 4 == r, pltpu.roll(x, 4 * r + 2, 1), side[k])
+    def put(k, r, x0, x1):
+        vecs[k][r + 2] = x0
+        vecs[k][r + 3] = x1
+        side[k] = jnp.where(
+            lane // 4 == r,
+            pltpu.roll(x0, 4 * r + 2, 1),
+            jnp.where(lane // 4 == r + 1, pltpu.roll(x1, lax.rem(4 * r + 6, cols), 1), side[k]),
+        )
 
     def pulled(t, p):
         flat = held.at[t].reshape(count * 8, cols)
@@ -202,8 +207,7 @@
             pull, low, preferred_element_type=jnp.float32
         )
         r = 8 * t + 2 * p
-        put(0, r, b[:, :cols])
-        put(0, r + 1, b[:, cols:])
+        put(0, r, b[:, :cols], b[:, cols:])
 
     side[0] = jnp.zeros((ND, cols), jnp.float32)
     for n, t in enumerate(order):
@@ -234,6 +238,26 @@
             jnp.where(lane == 0, y, x), cols - 1, 1
         )
 
+    source = lax.broadcasted_iota(jnp.int32, (cols, 2 * cols), 0)
+    target = lax.broadcasted_iota(jnp.int32, (cols, 2 * cols), 1)
+    first = target < cols
+    target = jnp.where(first, target, target - cols)
+
+    def band(gap):
+        near = jnp.where(gap == 1, jnp.where(first, 1.0, -8.0), 0.0)
+        return near + jnp.where(
+            first, 0.0, jnp.where(gap == 2, 1.0, jnp.where(gap == 0, 20.0, 0.0))
+        )
+
+    within = band(jnp.abs(source - target))
+    outer = jnp.where(
+        source >= cols - 2,
+        band(jnp.abs(source - cols - target)),
+        jnp.where(source < 2, band(jnp.abs(source + cols - target)), 0.0),
+    )
+    inner_bands = jnp.concatenate([within, within], axis=0).astype(jnp.bfloat16)
+    outer_bands = jnp.concatenate([outer, outer], axis=0).astype(jnp.bfloat16)
+
     for k in range(ITERS):
         v = vecs[k]
         last = k == ITERS - 1
@@ -242,30 +266,56 @@
         def _(p):
             r = 2 * p
             x = jnp.concatenate([v[r + 2], v[r + 3]], axis=1)
-            both = jnp.concatenate(split(x), axis=0)
-            y = jnp.dot(normal, both, preferred_element_type=jnp.float32)
+            high, low = split(x)
+            y = jnp.dot(
+                normal, jnp.concatenate([high, low], axis=0), preferred_element_type=jnp.float32
+            )
             y = (y[:ND] + y[ND:]) * (1.0 / scale)
-            temp[r] = y[:, :cols]
-            temp[r + 1] = y[:, cols:]
+            near = jnp.dot(
+                jnp.concatenate(
+                    [
+                        jnp.concatenate([high[:, :cols], low[:, :cols]], axis=1),
+                        jnp.concatenate([high[:, cols:], low[:, cols:]], axis=1),
+                    ],
+                    axis=0,
+                ),
+                inner_bands,
+                preferred_element_type=jnp.float32,
+            )
+            for j in range(2):
+                here = near[j * ND : (j + 1) * ND]
+                beside[r + j + 1] = here[:, :cols]
+                temp[r + j] = (
+                    y[:, j * cols : (j + 1) * cols]
+                    + k2 * here[:, cols:]
+                    - (shift / scale + k2 * col_out) * x[:, j * cols : (j + 1) * cols]
+                )
+
+        for r, at_edge in ((0, row == 0), (rows - 1, row == n_row - 1)):
+            @pl.when(at_edge)
+            def _():
+                temp[r] = temp[r] - k2 * v[r + 2]
 
         receive(k, (2, 3))
         side_in = jnp.where(lax.rem(lane, 4) < 2, from_left[k], from_right[k])
-        from_left[k] = side_in
-
-        @pl.loop(0, rows, unroll=4)
-        def _(r):
-            x = v[r + 2]
-            y = pltpu.roll(from_left[k], lax.rem(2 * cols - 2 - 4 * r, cols), 1)
-            h = horizontal(x, y)
-            d2 = pltpu.roll(jnp.where(lane >= cols - 2, y, x), 2, 1) + pltpu.roll(
-                jnp.where(lane < 2, y, x), cols - 2, 1
-            )
-            edge = jnp.where(jnp.logical_and(r == 0, row == 0), 1.0, 0.0) + jnp.where(
-                jnp.logical_and(r == rows - 1, row == n_row - 1), 1.0, 0.0
-            )
-            centre = (20.0 * k2 - shift / scale) - k2 * (col_out + edge)
-            beside[r + 1] = h
-            temp[r] = temp[r] + centre * x + k2 * (d2 - 8.0 * h)
+
+        group = 4
+
+        @pl.loop(0, rows // group, unroll=2)
+        def _(g):
+            start = group * g
+            lhs = []
+            for j in range(group):
+                y = pltpu.roll(side_in, lax.rem(2 * cols - 2 - 4 * (start + j), cols), 1)
+                lhs.append(jnp.concatenate(split(y), axis=1))
+            both = jnp.dot(
+                jnp.concatenate(lhs, axis=0), outer_bands, preferred_element_type=jnp.float32
+            )
+            for j in range(group):
+                r = start + j
+                got = both[j * ND : (j + 1) * ND]
+                beside[r + 1] += got[:, :cols]
+                temp[r] += k2 * got[:, cols:]
 
         receive(k, (0, 1, 4, 5, 6, 7))
         for at, h_at, left, right, a, b in (
@@ -296,8 +346,7 @@
             acc[2 * k + 1] += folded(x[2] * new[0] + x[3] * new[1])
             if not last:
                 acc[2 * k + 2] += folded(new[0] * new[0] + new[1] * new[1])
-                put(k + 1, r, new[0])
-                put(k + 1, r + 1, new[1])
+                put(k + 1, r, new[0], new[1])
 
         @pl.loop(0, 2)
         def _(e):

time: 50.9 us -> 44.4 us (0.87)
  Pallas kernels: 48.7 us -> 42.2 us
    pallas_call x1, Pallas kernels: 48.7 us -> 42.2 us  [on_device(): pl.pallas_call(functools.partial(kernel, (n_row, n_col, count, rows, cols...]
where the time goes in v2:
time: 44.4 us; the launch traced here: 44.2 us
  Pallas kernels  42.2 us (95%)
  local copies, waits for them, and re-layouts  2.01 us (5%)
    pallas_call x1, Pallas kernels, on_device(): pl.pallas_call(functools.partial(kernel, (n_row, n_col, count, rows, cols...  42.2 us
    unnamed x3, local copies, waits for them, and re-layouts  2.01 us

profile of v2, /device:TPU:0, one launch (start us, length us, event | category | flops | bytes accessed | tf_op | source)
XLA Modules:
  0.0 44.2 jit_solution(10908181361201320076)
XLA Ops:
  0.0 0.0 copy-start
  0.0 0.7 %copy-done = s32[512,2]{0,1:T(2,128)S(1)} copy-done((s32[512,2]{0,1:T(2,128)S(1)}, s32[512,2]{0,1:T(2,128)}, u32[]{:S(2)}) %copy-start) | copy-done | bytes 4120
  0.7 42.2 %shard_map.28 = f32[4096,128]{1,0:T(8,128)S(1)} custom-call(f32[512,4,8,128]{3,2,1,0:T(8,128)} %bitcast.5, s32[2,512]{1,0:T(2,128)S(1)} %bitcast.4), custom_call_target="tpu_custom_call" | custom-call | tf_op jit(solution)/shard_map/pallas_call | solution.py:412
  42.9 1.3 %copy.4 = f32[128,32,128]{2,1,0:T(8,128)} copy(f32[128,32,128]{2,1,0:T(8,128)S(1)} %bitcast.3) | data formatting | bytes 4194304
Async XLA Ops:
  0.0 0.7 %copy-start = (s32[512,2]{0,1:T(2,128)S(1)}, s32[512,2]{0,1:T(2,128)}, u32[]{:S(2)}) copy-start(s32[512,2]{0,1:T(2,128)} %param.3) | copy-start | bytes 12292
